TPU v7x, 256 devices: a whole 4x4x8 slice. The times are simulated.
256 devices in a mesh: kern: 4 (over z_lo, core), slab: 64 (over z_hi, y, x).
Axes of the slice: x: 4, y: 4, z: 8 (z_hi: 4, z_lo: 2; z = z_hi * 2 + z_lo), core: 2. Of those that a mesh axis runs over, the one named last changes fastest.
Arguments:
- layout: int32 [4096, 4096], P('slab', 'kern'), may hold values 0 or 1
- band_freqs: int32 [128], replicated, may hold values from -256 to 255, as said below
- kernels: float32 [2, 48, 128, 128], P(None, 'kern'), may hold values from -6 to 6
- eigen_values: float32 [48], P('kern'), may hold values from 0.1 to 1
- bake_rates: float32 [5], replicated, may hold values from 0.1 to 0.25
Outputs:
- aerial_image: float32 [4096, 4096], P('slab', 'kern')
- latent_acid: float32 [4096, 4096], P('slab', 'kern')
Inputs may be any that keep to these rules, and one draw needn't show every extreme that they name: `band_freqs`: the 128 numbers are distinct; both ends of the range are among them.
All inputs are finite; a program needn't handle non-finite values. No bound on the sum of `layout` on one device may be relied on, other than what follows from the above.
Results may differ from a plain program's by a relative error of at most 0.0017.
Values sent between devices are 32-bit elements; how exact they have to be, the bound alone decides.
No kernel may reach another device: no remote copies, remote signals or barrier semaphores. Data moves between devices by JAX's collectives and lax.ppermute only.
A program may use at most 64 MiB of HBM per device.

v0:
```python
import math
import jax
import jax.numpy as jnp
from jax import lax
from jax.sharding import PartitionSpec as P

N = 4096
W = 128
FIELDS = 48
STEPS = 2
highest = lax.Precision.HIGHEST


def padded_2(cells, sides, width):
    for axis, dim in sides:
        count = lax.axis_size(axis)
        head = lax.slice_in_dim(cells, 0, width, axis=dim)
        tail = lax.slice_in_dim(cells, cells.shape[dim] - width, cells.shape[dim], axis=dim)
        cells = jnp.concatenate(
            [
                lax.ppermute(tail, axis, [(i, (i + 1) % count) for i in range(count)]),
                cells,
                lax.ppermute(head, axis, [((i + 1) % count, i) for i in range(count)]),
            ],
            axis=dim,
        )
    return cells


def tables(frequencies, first_index, length):
    positions = first_index + jnp.arange(length, dtype=jnp.int32)
    angles = jnp.mod(positions[:, None] * frequencies[None, :], N).astype(jnp.float32) * (
        2.0 * math.pi / N
    )
    return (jnp.cos(angles), jnp.sin(angles))


def stencil(padded):
    centre = padded[:, 1:-1, 1:-1]
    return (
        padded[:, 2:, 1:-1]
        + padded[:, :-2, 1:-1]
        + padded[:, 1:-1, 2:]
        + padded[:, 1:-1, :-2]
        - 4.0 * centre
    )


def bake(aerial_image, bake_rates, extend):
    dill_rate, acid_rate, quench_rate, react_rate, quench_start = (
        bake_rates[0],
        bake_rates[1],
        bake_rates[2],
        bake_rates[3],
        bake_rates[4],
    )
    acid_field = 1.0 - jnp.exp(-4.0 * dill_rate * aerial_image)
    acid_diffusion = acid_rate * (0.5 + 0.5 * acid_field)
    quencher = jnp.zeros_like(acid_field) + quench_start
    for bake_step in range(STEPS):
        laplaces = stencil(extend(jnp.stack([acid_field, quencher])))
        reaction = 4.0 * react_rate * acid_field * quencher
        new_acid = acid_field + acid_diffusion * laplaces[0] - reaction
        quencher = quencher + quench_rate * laplaces[1] - reaction
        acid_field = new_acid
    return acid_field


def shards(layout, band_freqs, kernels, eigen_values, bake_rates):
    rows = layout.shape[0]
    cols = layout.shape[1]
    row_first = lax.axis_index("slab") * rows
    col_first = lax.axis_index("kern") * cols
    transmit = (2 * layout - 1).astype(jnp.float32)
    cos_col, sin_col = tables(band_freqs, col_first, cols)
    along_re = jnp.dot(transmit, cos_col, precision=highest)
    along_im = -jnp.dot(transmit, sin_col, precision=highest)
    cos_row, sin_row = tables(band_freqs, row_first, rows)
    first = (
        jnp.dot(cos_row.T, along_re, precision=highest)
        + jnp.dot(sin_row.T, along_im, precision=highest)
    ) / N
    second = (
        jnp.dot(cos_row.T, along_im, precision=highest)
        - jnp.dot(sin_row.T, along_re, precision=highest)
    ) / N
    spectrum = lax.psum(jnp.stack([first, second]), ("kern", "slab"))
    spec_re = spectrum[0]
    spec_im = spectrum[1]
    row_table = jnp.concatenate([cos_row, sin_row], 1).astype(jnp.bfloat16)
    cos_all, sin_all = tables(band_freqs, 0, N)
    col_table = jnp.concatenate(
        [jnp.concatenate([cos_all.T, sin_all.T], 1), jnp.concatenate([-sin_all.T, cos_all.T], 1)], 0
    ).astype(jnp.bfloat16)

    def one_field(total_sum, field_item):
        kern_re, kern_im, eigen_one = field_item
        prod_re = spec_re * kern_re - spec_im * kern_im
        prod_im = spec_re * kern_im + spec_im * kern_re
        spectral_block = jnp.concatenate(
            [jnp.concatenate([prod_re, prod_im], 1), jnp.concatenate([-prod_im, prod_re], 1)], 0
        ).astype(jnp.bfloat16)
        row_field = (
            jnp.dot(row_table, spectral_block, preferred_element_type=jnp.float32) / W
        ).astype(jnp.bfloat16)
        field_pair = jnp.dot(row_field, col_table, preferred_element_type=jnp.float32)
        power = field_pair[:, :N] * field_pair[:, :N] + field_pair[:, N:] * field_pair[:, N:]
        return (total_sum + eigen_one * power, None)

    partial_sum, unused = lax.scan(
        one_field, jnp.zeros((rows, N), jnp.float32), (kernels[0], kernels[1], eigen_values)
    )
    whole_image = lax.psum(partial_sum, "kern") / FIELDS

    def extend_rows(stacked):
        padded = padded_2(stacked, (("slab", 1),), 1)
        return jnp.concatenate([padded[:, :, -1:], padded, padded[:, :, :1]], 2)

    whole_acid = bake(whole_image, bake_rates, extend_rows)
    aerial_image = lax.dynamic_slice_in_dim(whole_image, col_first, cols, 1)
    latent_acid = lax.dynamic_slice_in_dim(whole_acid, col_first, cols, 1)
    return (aerial_image, latent_acid)


def solution(mesh):
    return jax.shard_map(
        shards,
        mesh=mesh,
        in_specs=(P("slab", "kern"), P(), P(None, "kern", None, None), P("kern"), P()),
        out_specs=(P("slab", "kern"), P("slab", "kern")),
        check_vma=False,
    )
```

profile of v0, /device:TPU:32, one launch (start us, length us, event | category | flops | bytes accessed | tf_op | source)
XLA Modules:
  0.0 427.2 jit_solution(13018393930706624220)
XLA Ops:
  7.3 3.4 convolution_negate_fusion
  10.7 2.5 fusion.68
  16.3 9.7 %fusion.63 = (bf16[128,4096]{1,0:T(8,128)(2,1)S(1)}, bf16[128,4096]{1,0:T(8,128)(2,1)S(1)}, bf16[128,4096]{1,0:T(8,128)(2,1)}) fusion(s32[128]{0:T(128)S(1)} %copy-done.3), kind=kLoop, calls=%fused_computation.106 | loop fusion | flops 9437184 | bytes 3146240 | tf_op jit(solution)/shard_map/convert.11
  26.0 2.7 slice_bitcast_fusion.1
  28.6 12.2 %maximum_maximum_fusion = bf16[256,8192]{1,0:T(8,128)(2,1)} fusion(bf16[128,4096]{1,0:T(8,128)(2,1)} %get-tuple-element.122, bf16[128,4096]{1,0:T(8,128)(2,1)S(1)} %get-tuple-element.121, bf16[128,4096]{1,0:T(8,128)(2,1)S(1)} %get-tuple-element.120), kind=kLoop, calls=%fused_computation.26 | loop fusion | flops 16777216 | bytes 7340032 | tf_op jit(solution)/shard_map/concatenate | solution.py:92
  40.8 222.1 %all-reduce.4.cloned.1.call-done = f32[2,128,128]{2,1,0:T(8,128)} async-done(((f32[2,128,128]{2,1,0:T(8,128)}), f32[2,128,128]{2,1,0:T(8,128)}) %all-reduce.4.cloned.1.call-update) | async-done | bytes 131088 | tf_op jit(solution)/shard_map/psum | solution.py:87
  263.8 72.9 %while.11 = (s32[]{:T(128)}, f32[64,4096]{1,0:T(8,128)S(1)}, f32[12]{0:T(128)S(1)}, f32[12,128,128]{2,1,0:T(8,128)}, f32[128,128]{1,0:T(8,128)S(1)}, /*index=5*/...) while((s32[]{:T(128)}, f32[64,4096]{1,0:T(8,128)S(1)}, ...), condition=%wide.region_2.3_spmd.clone, body=%wide.region_1.2_spmd.clone.sunk | while | flops 279117824 | bytes 11108491 | solution.py:110
  264.8 3.3 fusion.143
  270.8 3.3 fusion.143
  276.9 3.3 fusion.143
  283.0 3.3 fusion.143
  289.1 3.3 fusion.143
  295.1 3.3 fusion.143
  301.2 3.3 fusion.143
  307.3 3.3 fusion.143
  313.3 3.3 fusion.143
  319.4 3.3 fusion.143
  325.5 3.3 fusion.143
  331.6 3.3 fusion.143
  339.1 42.2 %all-reduce.6.cloned.1.call-done = f32[64,4096]{1,0:T(8,128)} async-done(((f32[64,4096]{1,0:T(8,128)}), f32[64,4096]{1,0:T(8,128)}) %all-reduce.6.cloned.1.call-update) | async-done | bytes 1048592 | tf_op jit(solution)/shard_map/psum | solution.py:113
  384.1 7.9 %collective-permute-start = (f32[2,1,4096]{2,1,0:T(1,128)S(1)}, f32[2,1,4096]{2,1,0:T(1,128)S(1)}, u32[]{:S(2)}, u32[]{:S(2)}) collective-permute-start(f32[2,1,4096]{2,1,0:T(1,128)S(1)} %get-tuple-element.110), channel_id=1, source_target_pairs={{1,0},{2,1},{3,2},{4,3},{5,4},{6,5},{7,6},{8,7},{9,8},{10,9},{11,1... | collective-permute-start | bytes 98312 | tf_op jit(solution)/shard_map/ppermute | solution.py:23
  393.6 8.8 %collective-permute-done.1 = f32[2,1,4096]{2,1,0:T(1,128)S(1)} collective-permute-done((f32[2,1,4096]{2,1,0:T(1,128)S(1)}, f32[2,1,4096]{2,1,0:T(1,128)S(1)}, u32[]{:S(2)}, u32[]{:S(2)}) %collective-permute-start.1) | collective-permute-done | bytes 32800 | tf_op jit(solution)/shard_map/ppermute | solution.py:21
  402.5 2.5 fusion.31
  411.5 6.4 %collective-permute-done.3 = f32[2,1,4096]{2,1,0:T(1,128)S(1)} collective-permute-done((f32[2,1,4096]{2,1,0:T(1,128)S(1)}, f32[2,1,4096]{2,1,0:T(1,128)S(1)}, u32[]{:S(2)}, u32[]{:S(2)}) %collective-permute-start.3) | collective-permute-done | bytes 32800 | tf_op jit(solution)/shard_map/ppermute | solution.py:21
  (89 shorter events, 51.0 us)
Async XLA Ops:
  7.2 3.5 copy-start.4
  7.2 3.5 copy-start.3
  7.2 255.8 %all-reduce.4.cloned.1.call-start = ((), (), s32[]{:S(2)}) async-start(), calls=%async_computation | async-start | bytes 262144 | tf_op jit(solution)/shard_map/psum | solution.py:87
  15.8 365.5 %all-reduce.6.cloned.1.call-start = ((), (), s32[]{:S(2)}) async-start(), calls=%async_computation.1 | async-start | bytes 2097152 | tf_op jit(solution)/shard_map/psum | solution.py:113
  28.6 235.2 %copy-start.5 = (f32[12]{0:T(128)S(1)}, f32[12]{0:T(128)}, u32[]{:S(2)}) copy-start(f32[12]{0:T(128)} %param.10) | copy-start | bytes 148
  263.8 73.9 %copy-start.2 = (f32[5]{0:T(128)S(1)}, f32[5]{0:T(128)}, u32[]{:S(2)}) copy-start(f32[5]{0:T(128)} %param.11) | copy-start | bytes 64
  336.7 1.0 copy-start
  384.1 9.5 %collective-permute-start = (f32[2,1,4096]{2,1,0:T(1,128)S(1)}, f32[2,1,4096]{2,1,0:T(1,128)S(1)}, u32[]{:S(2)}, u32[]{:S(2)}) collective-permute-start(f32[2,1,4096]{2,1,0:T(1,128)S(1)} %get-tuple-element.110), channel_id=1, source_target_pairs={{1,0},{2,1},{3,2},{4,3},{5,4},{6,5},{7,6},{8,7},{9,8},{10,9},{11,1... | collective-permute-start | bytes 98312 | tf_op jit(solution)/shard_map/ppermute | solution.py:23
  392.0 10.4 %collective-permute-start.1 = (f32[2,1,4096]{2,1,0:T(1,128)S(1)}, f32[2,1,4096]{2,1,0:T(1,128)S(1)}, u32[]{:S(2)}, u32[]{:S(2)}) collective-permute-start(f32[2,1,4096]{2,1,0:T(1,128)S(1)} %get-tuple-element.109), channel_id=1, source_target_pairs={{0,1},{1,2},{2,3},{3,4},{4,5},{5,6},{6,7},{7,8},{8,9},{9,10},{10,1... | collective-permute-start | bytes 98312 | tf_op jit(solution)/shard_map/ppermute | solution.py:21
  393.4 11.6 %copy-start.1 = (f32[64,4096]{1,0:T(8,128)S(1)}, f32[64,4096]{1,0:T(8,128)}, u32[]{:S(2)}) copy-start(f32[64,4096]{1,0:T(8,128)} %all-reduce.6.cloned.1.call-done) | copy-start | bytes 3145732
  407.5 4.0 collective-permute-start.2
  407.6 10.3 %collective-permute-start.3 = (f32[2,1,4096]{2,1,0:T(1,128)S(1)}, f32[2,1,4096]{2,1,0:T(1,128)S(1)}, u32[]{:S(2)}, u32[]{:S(2)}) collective-permute-start(f32[2,1,4096]{2,1,0:T(1,128)S(1)} %get-tuple-element.103), channel_id=1, source_target_pairs={{0,1},{1,2},{2,3},{3,4},{4,5},{5,6},{6,7},{7,8},{8,9},{9,10},{10,1... | collective-permute-start | bytes 98312 | tf_op jit(solution)/shard_map/ppermute | solution.py:21
Sparse Core Ops, SparseCore 0:
  15.9 246.9 all-reduce.3
  337.8 43.4 all-reduce.5
where the time goes:
time: 429 us; the launch traced here: 427 us
  waiting for transfers between devices  281 us (66%)
  other arithmetic  58.7 us (14%)
  matrix products  47.6 us (11%)
  between operations  15.6 us (4%)
  local copies, waits for them, and re-layouts  13.8 us (3%)
  starting transfers between devices  10.2 us (2%)
    psum x1, waiting for transfers between devices, shards(): spectrum = lax.psum(jnp.stack([first, second]), ('kern', 'slab'))  222 us
    psum x1, waiting for transfers between devices, shards(): whole_image = lax.psum(partial_sum, 'kern') / FIELDS  42.2 us
    dot_general x12, matrix products, one_field(): jnp.dot(row_field, col_table, preferred_element_type=jnp.float32)  39.8 us
    another operation x26, other arithmetic  20.8 us
    ppermute x2, waiting for transfers between devices, padded_2(): lax.ppermute(tail, axis, [(i, (i + 1) % count) for i in range(count)])  15.3 us
    add x12, other arithmetic, one_field(): return (total_sum + eigen_one * power, None)  14.7 us
    concatenate x1, other arithmetic, shards(): jnp.concatenate([jnp.concatenate([cos_all.T, sin_all.T], 1), jnp.concaten...  12.2 us
  transfers between devices with their start and end apart: 6, of which 6 were waited for; matrix products, arithmetic and copies ran while one was open for 6% of the time, Pallas kernels for 0%

commit v1 on v0

--- a/solution.py
+++ b/solution.py
@@ -9,6 +9,7 @@
 FIELDS = 48
 STEPS = 2
 highest = lax.Precision.HIGHEST
+end_view = lambda field: lax.psum(lax.psum(field, axis_name="slab"), axis_name="kern")
 
 
 def padded_2(cells, sides, width):
@@ -84,7 +85,7 @@
         jnp.dot(cos_row.T, along_im, precision=highest)
         - jnp.dot(sin_row.T, along_re, precision=highest)
     ) / N
-    spectrum = lax.psum(jnp.stack([first, second]), ("kern", "slab"))
+    spectrum = end_view(jnp.stack([first, second]))
     spec_re = spectrum[0]
     spec_im = spectrum[1]
     row_table = jnp.concatenate([cos_row, sin_row], 1).astype(jnp.bfloat16)

time: 429 us -> 879 us (2.05)
  waiting for transfers between devices: 281 us -> 727 us
    psum x1 -> x2, waiting for transfers between devices: 222 us -> 665 us  [the longest x1 626 us: lax.psum(field, axis_name='slab')]
  transfers between devices with their start and end apart: 6 -> 7, of which waited for: 6 -> 7; matrix products, arithmetic and copies ran while one was open for 6% -> 4% of each run, Pallas kernels for 0% -> 0%
where the time goes in v1:
time: 879 us; the launch traced here: 878 us
  waiting for transfers between devices  727 us (83%)
  other arithmetic  64.4 us (7%)
  matrix products  47.6 us (5%)
  between operations  15.3 us (2%)
  local copies, waits for them, and re-layouts  12.4 us (1%)
  starting transfers between devices  10.5 us (1%)
    psum x1, waiting for transfers between devices, lax.psum(field, axis_name='slab')  626 us
    psum x1, waiting for transfers between devices, shards(): whole_image = lax.psum(partial_sum, 'kern') / FIELDS  45.7 us
    dot_general x12, matrix products, one_field(): jnp.dot(row_field, col_table, preferred_element_type=jnp.float32)  39.8 us
    psum x1, waiting for transfers between devices, lax.psum(lax.psum(field, axis_name='slab'), axis_name='kern')  38.7 us
    another operation x26, other arithmetic  20.1 us
    concatenate x1, other arithmetic, shards(): jnp.concatenate([jnp.concatenate([cos_all.T, sin_all.T], 1), jnp.concaten...  18.6 us
  transfers between devices with their start and end apart: 7, of which 7 were waited for; matrix products, arithmetic and copies ran while one was open for 4% of the time, Pallas kernels for 0%

profile of v1, /device:TPU:32, one launch (start us, length us, event | category | flops | bytes accessed | tf_op | source)
XLA Modules:
  0.0 878.0 jit_solution(6567416712568292578)
XLA Ops:
  7.2 3.4 convolution_negate_fusion
  10.7 2.5 fusion.68
  16.0 9.0 %fusion.63 = (bf16[128,4096]{1,0:T(8,128)(2,1)S(1)}, bf16[128,4096]{1,0:T(8,128)(2,1)S(1)}, bf16[128,4096]{1,0:T(8,128)(2,1)S(1)}) fusion(s32[128]{0:T(128)S(1)} %copy-done.4), kind=kLoop, calls=%fused_computation.106 | loop fusion | flops 9437184 | bytes 3146240 | tf_op jit(solution)/shard_map/convert.11
  25.1 18.6 %maximum_maximum_fusion = bf16[256,8192]{1,0:T(8,128)(2,1)} fusion(bf16[128,4096]{1,0:T(8,128)(2,1)S(1)} %get-tuple-element.122, bf16[128,4096]{1,0:T(8,128)(2,1)S(1)} %get-tuple-element.121, bf16[128,4096]{1,0:T(8,128)(2,1)S(1)} %get-tuple-element.120), kind=kLoop, calls=%fused_computation.26 | loop fusion | flops 16777216 | bytes 7340032 | tf_op jit(solution)/shard_map/concatenate | solution.py:93
  45.0 626.4 %all-reduce.5.cloned.1.call-done = f32[2,128,128]{2,1,0:T(8,128)} async-done(((f32[2,128,128]{2,1,0:T(8,128)}), f32[2,128,128]{2,1,0:T(8,128)}) %all-reduce.5.cloned.1.call-update) | async-done | bytes 131088 | tf_op jit(solution)/shard_map/psum | solution.py:12
  671.9 38.7 %all-reduce.7.cloned.1.call-done = f32[2,128,128]{2,1,0:T(8,128)} async-done(((f32[2,128,128]{2,1,0:T(8,128)}), f32[2,128,128]{2,1,0:T(8,128)}) %all-reduce.7.cloned.1.call-update) | async-done | bytes 131088 | tf_op jit(solution)/shard_map/psum | solution.py:12
  711.5 72.8 %while.11 = (s32[]{:T(128)}, f32[64,4096]{1,0:T(8,128)S(1)}, f32[12]{0:T(128)S(1)}, f32[12,128,128]{2,1,0:T(8,128)}, f32[128,128]{1,0:T(8,128)S(1)}, /*index=5*/...) while((s32[]{:T(128)}, f32[64,4096]{1,0:T(8,128)S(1)}, ...), condition=%wide.region_3.4_spmd.clone, body=%wide.region_2.3_spmd.clone.sunk | while | flops 279117824 | bytes 11108491 | solution.py:111
  712.5 3.3 fusion.143
  718.5 3.3 fusion.143
  724.6 3.3 fusion.143
  730.7 3.3 fusion.143
  736.7 3.3 fusion.143
  742.8 3.3 fusion.143
  748.9 3.3 fusion.143
  754.9 3.3 fusion.143
  761.0 3.3 fusion.143
  767.1 3.3 fusion.143
  773.1 3.3 fusion.143
  779.2 3.3 fusion.143
  786.7 45.7 %all-reduce.9.cloned.1.call-done = f32[64,4096]{1,0:T(8,128)} async-done(((f32[64,4096]{1,0:T(8,128)}), f32[64,4096]{1,0:T(8,128)}) %all-reduce.9.cloned.1.call-update) | async-done | bytes 1048592 | tf_op jit(solution)/shard_map/psum | solution.py:114
  835.2 7.9 collective-permute-start
  844.7 8.8 %collective-permute-done.1 = f32[2,1,4096]{2,1,0:T(1,128)S(1)} collective-permute-done((f32[2,1,4096]{2,1,0:T(1,128)S(1)}, f32[2,1,4096]{2,1,0:T(1,128)S(1)}, u32[]{:S(2)}, u32[]{:S(2)}) %collective-permute-start.1) | collective-permute-done | bytes 32800 | tf_op jit(solution)/shard_map/ppermute | solution.py:22
  853.6 2.5 fusion.31
  862.6 6.4 collective-permute-done.3
  (94 shorter events, 52.5 us)
Async XLA Ops:
  7.2 3.5 copy-start.5
  7.2 3.5 copy-start.4
  7.2 664.2 %all-reduce.5.cloned.1.call-start = ((), (), s32[]{:S(2)}) async-start(), calls=%async_computation | async-start | bytes 262144 | tf_op jit(solution)/shard_map/psum | solution.py:12
  15.8 694.8 %all-reduce.7.cloned.1.call-start = ((), (), s32[]{:S(2)}) async-start(), calls=%async_computation.1 | async-start | bytes 262144 | tf_op jit(solution)/shard_map/psum | solution.py:12
  25.1 18.6 %copy-start.2 = (f32[2,12,128,128]{3,2,1,0:T(8,128)S(1)}, f32[2,12,128,128]{3,2,1,0:T(8,128)}, u32[]{:S(2)}) copy-start(f32[2,12,128,128]{3,2,1,0:T(8,128)} %param.9) | copy-start | bytes 4718596
  43.7 667.8 %copy-start.6 = (f32[12]{0:T(128)S(1)}, f32[12]{0:T(128)}, u32[]{:S(2)}) copy-start(f32[12]{0:T(128)} %param.10) | copy-start | bytes 148
  671.4 161.1 %all-reduce.9.cloned.1.call-start = ((), (), s32[]{:S(2)}) async-start(), calls=%async_computation.2 | async-start | bytes 2097152 | tf_op jit(solution)/shard_map/psum | solution.py:114
  711.5 73.8 %copy-start.3 = (f32[5]{0:T(128)S(1)}, f32[5]{0:T(128)}, u32[]{:S(2)}) copy-start(f32[5]{0:T(128)} %param.11) | copy-start | bytes 64
  784.4 1.0 copy-start
  835.2 9.5 %collective-permute-start = (f32[2,1,4096]{2,1,0:T(1,128)S(1)}, f32[2,1,4096]{2,1,0:T(1,128)S(1)}, u32[]{:S(2)}, u32[]{:S(2)}) collective-permute-start(f32[2,1,4096]{2,1,0:T(1,128)S(1)} %get-tuple-element.110), channel_id=1, source_target_pairs={{1,0},{2,1},{3,2},{4,3},{5,4},{6,5},{7,6},{8,7},{9,8},{10,9},{11,1... | collective-permute-start | bytes 98312 | tf_op jit(solution)/shard_map/ppermute | solution.py:24
  843.1 10.4 %collective-permute-start.1 = (f32[2,1,4096]{2,1,0:T(1,128)S(1)}, f32[2,1,4096]{2,1,0:T(1,128)S(1)}, u32[]{:S(2)}, u32[]{:S(2)}) collective-permute-start(f32[2,1,4096]{2,1,0:T(1,128)S(1)} %get-tuple-element.109), channel_id=1, source_target_pairs={{0,1},{1,2},{2,3},{3,4},{4,5},{5,6},{6,7},{7,8},{8,9},{9,10},{10,1... | collective-permute-start | bytes 98312 | tf_op jit(solution)/shard_map/ppermute | solution.py:22
  844.6 11.5 %copy-start.1 = (f32[64,4096]{1,0:T(8,128)S(1)}, f32[64,4096]{1,0:T(8,128)}, u32[]{:S(2)}) copy-start(f32[64,4096]{1,0:T(8,128)} %all-reduce.9.cloned.1.call-done) | copy-start | bytes 3145732
  858.6 4.0 collective-permute-start.2
  858.7 10.3 %collective-permute-start.3 = (f32[2,1,4096]{2,1,0:T(1,128)S(1)}, f32[2,1,4096]{2,1,0:T(1,128)S(1)}, u32[]{:S(2)}, u32[]{:S(2)}) collective-permute-start(f32[2,1,4096]{2,1,0:T(1,128)S(1)} %get-tuple-element.103), channel_id=1, source_target_pairs={{0,1},{1,2},{2,3},{3,4},{4,5},{5,6},{6,7},{7,8},{8,9},{9,10},{10,1... | collective-permute-start | bytes 98312 | tf_op jit(solution)/shard_map/ppermute | solution.py:22
Sparse Core Ops, SparseCore 0:
  15.9 655.3 all-reduce.4
  674.0 36.6 all-reduce.6
  785.5 46.8 all-reduce.8
